TPU v7x, 32 devices: a whole 2x2x4 slice. The times are simulated.
32 devices in a mesh: dp: 8 (over y, x, core), mp: 4 (over z).
Axes of the slice: x: 2, y: 2, z: 4, core: 2. Of those that a mesh axis runs over, the one named last changes fastest.
Arguments:
- patches: bfloat16 [1024, 6144], P('dp', 'mp'), may hold values from -64 to 64
- send_start: int32 [8, 8], P('dp'), may hold values from 0 to 128, as said below
- run_length: int32 [8, 8], P('dp'), may hold values from 0 to 32, as said below
- slot_start: int32 [8, 8], P('dp'), may hold values from 0 to 128, as said below
- image_ids: int32 [8, 128], P('dp'), may hold values from 0 to 7, never falling along the last dimension, each value on 1 to 32 neighbouring positions
- norm_gain: float32 [6144], replicated, may hold values from 0.1 to 1.9
- qkv_weight: bfloat16 [6144, 3, 4096], P('dp', None, 'mp'), may hold values from -0.078125 to 0.078125
- query_gain: float32 [128], replicated, may hold values from 0.1 to 1.9
- key_gain: float32 [128], replicated, may hold values from 0.1 to 1.9
- out_weight: bfloat16 [4096, 6144], P('mp'), may hold values from -0.09375 to 0.09375
Outputs:
- packed: bfloat16 [1024, 6144], P('dp', 'mp')
- attended: bfloat16 [1024, 6144], P('dp', 'mp')
Inputs may be any that keep to these rules, and one draw needn't show every extreme that they name: `run_length`: every source's runs sum to 128 and every pack's runs sum to 128; the longest run is exactly 32. `send_start`: the runs of one source device do not intersect and cover its 128 rows. `slot_start`: the runs into one pack do not intersect and fill its 128 slots. `image_ids`: image numbers never fall along a pack; equal numbers mark one image.
All inputs are finite; a program needn't handle non-finite values.
Results may differ from a plain program's by a relative error of at most 0.011.
Values may be sent and summed in bfloat16 or wider, within the bound.
A program may use at most 128 MiB of HBM per device.

v0:
```python
import jax
import jax.numpy as jnp
from jax import lax
from jax.sharding import PartitionSpec as P

epsilon = 1e-06


def row_norm(values, scales):
    middle = jnp.mean(values, axis=-1, keepdims=True)
    spread = jnp.mean(values * values, axis=-1, keepdims=True) - middle * middle
    return (values - middle) * lax.rsqrt(spread + epsilon) * scales


def on_device(
    patches,
    send_start,
    run_length,
    slot_start,
    image_ids,
    norm_gain,
    qkv_weight,
    query_gain,
    key_gain,
    out_weight,
):
    pack_rows, feat_local = patches.shape
    pack_count = lax.axis_size("dp")
    mp_count = lax.axis_size("mp")
    capacity = 2 * pack_rows // pack_count
    local_cols = qkv_weight.shape[1] * qkv_weight.shape[2]
    offsets = jnp.arange(capacity, dtype=jnp.int32)
    rows = jnp.arange(pack_rows, dtype=jnp.int32)
    x = patches.astype(jnp.float32)
    sums = jnp.stack([jnp.sum(x, axis=-1), jnp.sum(x * x, axis=-1)])
    sums = lax.psum(sums, "mp") / (feat_local * mp_count)
    middle = sums[0][:, None]
    spread = sums[1][:, None] - middle * middle
    gain = lax.dynamic_slice_in_dim(norm_gain, lax.axis_index("mp") * feat_local, feat_local)
    normed = ((x - middle) * lax.rsqrt(spread + epsilon) * gain).astype(jnp.bfloat16)
    wide = lax.all_gather(normed, "mp", axis=1, tiled=True)
    slices = lax.all_to_all(wide, "dp", split_axis=1, concat_axis=0, tiled=True)
    tables = jnp.concatenate([send_start, run_length, slot_start], axis=0)[None]
    tables = lax.all_gather(tables, "dp", axis=0, tiled=True)
    starts, lengths, slots = (tables[:, 0].T, tables[:, 1].T, tables[:, 2])
    inside = (rows >= slots[:, :, None]) & (rows < (slots + lengths)[:, :, None])
    base = jnp.arange(pack_count, dtype=jnp.int32)[None, :] * pack_rows + starts - slots
    origin = jnp.sum(jnp.where(inside, base[:, :, None] + rows, 0), axis=1).reshape(-1)
    chosen = (origin[:, None] == jnp.arange(origin.shape[0], dtype=jnp.int32)).astype(jnp.bfloat16)
    ordered = jnp.dot(chosen, slices, preferred_element_type=jnp.float32).astype(jnp.bfloat16)
    partial = jnp.dot(
        ordered,
        qkv_weight.reshape(qkv_weight.shape[0], local_cols),
        preferred_element_type=jnp.float32,
    ).astype(jnp.bfloat16)
    projected = lax.psum_scatter(partial, "dp", scatter_dimension=0, tiled=True).astype(jnp.float32)
    own_rows = send_start[0][:, None] + offsets[None, :]
    occupied = offsets[None, :] < run_length[0][:, None]
    pick = (occupied[:, :, None] & (own_rows[:, :, None] == rows)).astype(jnp.bfloat16)
    outgoing = jnp.dot(
        pick.reshape(-1, pack_rows), patches, preferred_element_type=jnp.float32
    ).astype(jnp.bfloat16)
    arrived = lax.all_to_all(
        outgoing.reshape(pack_count, capacity, feat_local),
        "dp",
        split_axis=0,
        concat_axis=0,
        tiled=True,
    )
    targets = (slot_start[0][:, None] + offsets[None, :]).reshape(-1)
    place = (rows[:, None] == targets[None, :]).astype(jnp.bfloat16)
    packed = jnp.dot(
        place, arrived.reshape(-1, feat_local), preferred_element_type=jnp.float32
    ).astype(jnp.bfloat16)
    head_size = query_gain.shape[0]
    heads_here = qkv_weight.shape[2] // head_size
    split_heads = projected.reshape(pack_rows, 3, heads_here, head_size)
    queries = row_norm(split_heads[:, 0], query_gain).astype(jnp.bfloat16)
    key_rows = row_norm(split_heads[:, 1], key_gain).astype(jnp.bfloat16)
    values = split_heads[:, 2].astype(jnp.bfloat16)
    scores = jnp.einsum(
        "qhd,khd->hqk", queries, key_rows, preferred_element_type=jnp.float32
    ) * head_size ** (-0.5)
    image_of = image_ids[0]
    same_image = image_of[:, None] == image_of[None, :]
    weights_raw = jnp.where(same_image[None], jnp.exp(scores), 0.0)
    totals = jnp.sum(weights_raw, axis=-1, keepdims=True)
    attention = (weights_raw / totals).astype(jnp.bfloat16)
    context = jnp.einsum(
        "hqk,khd->qhd", attention, values, preferred_element_type=jnp.float32
    ).astype(jnp.bfloat16)
    context = context.reshape(pack_rows, heads_here * head_size)
    partial_value = jnp.dot(context, out_weight, preferred_element_type=jnp.float32)
    attended = lax.psum_scatter(
        partial_value.astype(jnp.bfloat16), "mp", scatter_dimension=1, tiled=True
    )
    return (packed, attended)


def solution(mesh):
    return jax.shard_map(
        on_device,
        mesh=mesh,
        in_specs=(
            P("dp", "mp"),
            P("dp", None),
            P("dp", None),
            P("dp", None),
            P("dp", None),
            P(),
            P("dp", None, "mp"),
            P(),
            P(),
            P("mp", None),
        ),
        out_specs=(P("dp", "mp"), P("dp", "mp")),
        check_vma=False,
    )
```

profile of v0, /device:TPU:0, one launch (start us, length us, event | category | flops | bytes accessed | tf_op | source)
XLA Modules:
  0.0 220.3 jit_solution(4133471638652877734)
XLA Ops:
  7.2 1.2 copy.47
  8.7 13.5 %psum.7 = f32[2,128]{1,0:T(2,128)S(1)} all-reduce(f32[2,128]{1,0:T(2,128)S(1)} %pad_maximum_fusion), channel_id=1, replica_groups=mesh['dp'=8,'mp'=4] {'mp'}, use_global_device_ids=true, to_apply=%region_3.4 | all-reduce | flops 256 | bytes 2048 | tf_op jit(solution)/shard_map/psum | solution.py:36
  22.1 0.8 dynamic_slice.3
  22.9 1.0 fusion.8
  24.0 35.5 %all-gather.4.cloned.1.call-done = bf16[128,6144]{0,1:T(8,128)(2,1)} async-done(((bf16[128,1536]{0,1:T(8,128)(2,1)}), bf16[128,6144]{0,1:T(8,128)(2,1)}) %all-gather.4.cloned.1.call-update) | async-done | bytes 1572880 | tf_op jit(solution)/shard_map/all_gather | solution.py:41
  59.4 3.8 %all-to-all-start.1 = ((bf16[128,8,768]{0,2,1:T(8,128)(2,1)}), bf16[128,8,768]{0,2,1:T(8,128)(2,1)S(1)}, u32[]{:S(2)}, u32[]{:S(2)}) async-start(bf16[128,8,768]{0,2,1:T(8,128)(2,1)} %bitcast.83), calls=%async_computation.1 | async-start | bytes 3145728 | tf_op jit(solution)/shard_map/all_to_all | solution.py:42
  63.3 24.0 %all-gather.1 = s32[8,3,8]{2,1,0:T(4,128)S(1)} all-gather(s32[1,3,8]{2,1,0:T(4,128)S(1)} %add_bitcast_fusion), channel_id=2, replica_groups=mesh['dp'=8,'mp'=4] {'dp'}, dimensions={0}, use_global_device_ids=true | all-gather | bytes 864 | tf_op jit(solution)/shard_map/all_gather | solution.py:44
  87.5 6.7 %copy.49 = bf16[768,3,1024]{0,2,1:T(8,128)(2,1)} copy(bf16[768,3,1024]{2,0,1:T(8,128)(2,1)} %param.16) | data formatting | bytes 9437184 | tf_op args[6]
  94.3 0.7 copy.48
  95.0 12.2 %convolution_convert_fusion.1 = bf16[1024,3072]{1,0:T(8,128)(2,1)} fusion(bf16[768,3072]{0,1:T(8,128)(2,1)} %bitcast.79, bf16[1024,768]{1,0:T(8,128)(2,1)S(1)} %bitcast.84, s32[1024]{0:T(1024)S(1)} %bitcast.91), kind=kOutput, calls=%fused_computation.1 | convolution fusion | flops 6447431680 | bytes 12587008 | tf_op jit(solution)/shard_map/dot_general | solution.py:51
  107.4 0.6 copy-done.1
  108.0 59.1 %reduce-scatter.3.cloned.1.call-done = bf16[128,3072]{1,0:T(8,128)(2,1)} async-done(((bf16[1024,3072]{1,0:T(8,128)(2,1)}), bf16[128,3072]{1,0:T(8,128)(2,1)}) %reduce-scatter.3.cloned.1.call-update) | async-done | bytes 786448 | tf_op jit(solution)/shard_map/reduce_scatter | solution.py:56
  167.2 1.3 copy.58
  168.7 0.3 slice_reduce_fusion.1
  169.0 0.3 fusion.16
  169.7 0.7 fusion.4
  170.4 0.3 convolution_convert_fusion.4
  170.7 7.6 %convolution_convert_fusion = bf16[128,6144]{1,0:T(8,128)(2,1)} fusion(bf16[128,1024]{0,1:T(8,128)(2,1)S(1)} %bitcast.86, bf16[1024,6144]{1,0:T(8,128)(2,1)} %param.19), kind=kOutput, calls=%fused_computation | convolution fusion | flops 1611399168 | bytes 14417920 | tf_op jit(solution)/shard_map/dot_general | solution.py:93
  178.6 0.7 copy-done
  179.3 1.3 convolution_convert_fusion.2
  180.6 3.5 %all-to-all-start = ((bf16[8,32,1536]{2,1,0:T(8,128)(2,1)}), bf16[8,32,1536]{2,1,0:T(8,128)(2,1)S(1)}, u32[]{:S(2)}, u32[]{:S(2)}) async-start(bf16[8,32,1536]{2,1,0:T(8,128)(2,1)} %bitcast.3), calls=%async_computation | async-start | bytes 1572864 | tf_op jit(solution)/shard_map/all_to_all | solution.py:63
  184.3 12.4 %all-to-all-done = bf16[8,32,1536]{2,1,0:T(8,128)(2,1)S(1)} async-done(((bf16[8,32,1536]{2,1,0:T(8,128)(2,1)}), bf16[8,32,1536]{2,1,0:T(8,128)(2,1)S(1)}, u32[]{:S(2)}, u32[]{:S(2)}) %all-to-all-start) | async-done | bytes 786464 | tf_op jit(solution)/shard_map/all_to_all | solution.py:63
  196.7 1.0 convolution_convert_fusion.3
  197.7 16.0 %reduce-scatter.5.cloned.1.call-done = bf16[128,1536]{1,0:T(8,128)(2,1)} async-done(((bf16[128,6144]{1,0:T(8,128)(2,1)}), bf16[128,1536]{1,0:T(8,128)(2,1)}) %reduce-scatter.5.cloned.1.call-update) | async-done | bytes 393232 | tf_op jit(solution)/shard_map/reduce_scatter | solution.py:94
  (42 shorter events, 1.7 us)
Async XLA Ops:
  7.2 52.3 %all-gather.4.cloned.1.call-start = ((), (), s32[]{:S(2)}) async-start(), calls=%async_computation.4 | async-start | bytes 1966080 | tf_op jit(solution)/shard_map/all_gather | solution.py:41
  59.4 3.8 %copy-start.2 = (s32[1,8]{1,0:T(1,128)S(1)}, s32[1,8]{1,0:T(1,128)}, u32[]{:S(2)}) copy-start(s32[1,8]{1,0:T(1,128)} %param.11) | copy-start | bytes 100
  59.4 3.8 %copy-start.3 = (s32[1,8]{1,0:T(1,128)S(1)}, s32[1,8]{1,0:T(1,128)}, u32[]{:S(2)}) copy-start(s32[1,8]{1,0:T(1,128)} %param.13) | copy-start | bytes 100
  59.4 3.9 %copy-start.4 = (s32[1,8]{1,0:T(1,128)S(1)}, s32[1,8]{1,0:T(1,128)}, u32[]{:S(2)}) copy-start(s32[1,8]{1,0:T(1,128)} %param.12) | copy-start | bytes 100
  59.4 34.9 %all-to-all-start.1 = ((bf16[128,8,768]{0,2,1:T(8,128)(2,1)}), bf16[128,8,768]{0,2,1:T(8,128)(2,1)S(1)}, u32[]{:S(2)}, u32[]{:S(2)}) async-start(bf16[128,8,768]{0,2,1:T(8,128)(2,1)} %bitcast.83), calls=%async_computation.1 | async-start | bytes 3145728 | tf_op jit(solution)/shard_map/all_to_all | solution.py:42
  63.2 103.9 %reduce-scatter.3.cloned.1.call-start = ((), (), s32[]{:S(2)}) async-start(), calls=%async_computation.5 | async-start | bytes 7077888 | tf_op jit(solution)/shard_map/reduce_scatter | solution.py:56
  107.3 0.7 copy-start.1
  107.3 106.4 %reduce-scatter.5.cloned.1.call-start = ((), (), s32[]{:S(2)}) async-start(), calls=%async_computation.6 | async-start | bytes 1966080 | tf_op jit(solution)/shard_map/reduce_scatter | solution.py:94
  168.6 1.0 copy-start.5
  168.7 1.0 copy-start.6
  178.3 1.0 copy-start
  180.6 16.1 %all-to-all-start = ((bf16[8,32,1536]{2,1,0:T(8,128)(2,1)}), bf16[8,32,1536]{2,1,0:T(8,128)(2,1)S(1)}, u32[]{:S(2)}, u32[]{:S(2)}) async-start(bf16[8,32,1536]{2,1,0:T(8,128)(2,1)} %bitcast.3), calls=%async_computation | async-start | bytes 1572864 | tf_op jit(solution)/shard_map/all_to_all | solution.py:63
Sparse Core Ops, SparseCore 0:
  24.1 35.2 all-gather.3
  107.4 59.6 reduce-scatter.2
  178.4 35.2 reduce-scatter.4
where the time goes:
time: 221 us; the launch traced here: 220 us
  waiting for transfers between devices  123 us (56%)
  blocking collectives  37.5 us (17%)
  matrix products  23.2 us (10%)
  between operations  13.9 us (6%)
  local copies, waits for them, and re-layouts  12.6 us (6%)
  starting transfers between devices  7.45 us (3%)
  other arithmetic  2.56 us (1%)
    reduce_scatter x1, waiting for transfers between devices, on_device(): lax.psum_scatter(partial, 'dp', scatter_dimension=0, tiled=True)  59.1 us
    all_gather x1, waiting for transfers between devices, on_device(): wide = lax.all_gather(normed, 'mp', axis=1, tiled=True)  35.5 us
    all_gather x1, blocking collectives, on_device(): tables = lax.all_gather(tables, 'dp', axis=0, tiled=True)  24 us
    reduce_scatter x1, waiting for transfers between devices, on_device(): lax.psum_scatter(partial_value.astype(jnp.bfloat16), 'mp', scatter_dimens...  16 us
    psum x1, blocking collectives, on_device(): sums = lax.psum(sums, 'mp') / (feat_local * mp_count)  13.5 us
    all_to_all x1, waiting for transfers between devices, on_device(): lax.all_to_all(outgoing.reshape(pack_count, capacity, feat_local), 'dp',...  12.4 us
    dot_general x1, matrix products, on_device(): jnp.dot(ordered, qkv_weight.reshape(qkv_weight.shape[0], local_cols), pre...  12.2 us
    unnamed x18, local copies, waits for them, and re-layouts  10.7 us
  transfers between devices with their start and end apart: 5, of which 4 were waited for; matrix products, arithmetic and copies ran while one was open for 4% of the time, Pallas kernels for 0%

commit v1 on v0

--- a/solution.py
+++ b/solution.py
@@ -4,6 +4,25 @@
 from jax.sharding import PartitionSpec as P
 
 epsilon = 1e-06
+
+
+def in_order(blocks, dim):
+    lengths = list(blocks.shape[1:])
+    lengths[dim] *= blocks.shape[0]
+    return jnp.moveaxis(blocks, 0, dim).reshape(lengths)
+
+
+def grow_blocks(array, axis):
+    size, here = (lax.axis_size(axis), lax.axis_index(axis))
+    blocks, bit = (array[None], 1)
+    while bit < size:
+        partner_block = lax.ppermute(blocks, axis, [(i, i ^ bit) for i in range(size)])
+        low = here & bit == 0
+        blocks = jnp.concatenate(
+            [jnp.where(low, blocks, partner_block), jnp.where(low, partner_block, blocks)]
+        )
+        bit *= 2
+    return blocks
 
 
 def row_norm(values, scales):
@@ -41,7 +60,7 @@
     wide = lax.all_gather(normed, "mp", axis=1, tiled=True)
     slices = lax.all_to_all(wide, "dp", split_axis=1, concat_axis=0, tiled=True)
     tables = jnp.concatenate([send_start, run_length, slot_start], axis=0)[None]
-    tables = lax.all_gather(tables, "dp", axis=0, tiled=True)
+    tables = in_order(grow_blocks(tables, "dp"), 0)
     starts, lengths, slots = (tables[:, 0].T, tables[:, 1].T, tables[:, 2])
     inside = (rows >= slots[:, :, None]) & (rows < (slots + lengths)[:, :, None])
     base = jnp.arange(pack_count, dtype=jnp.int32)[None, :] * pack_rows + starts - slots

time: 221 us -> 218 us (0.986)
  blocking collectives: 37.5 us -> 13.5 us
  waiting for transfers between devices: 123 us -> 140 us
  starting transfers between devices: 7.45 us -> 11 us
    all_gather x1 -> x0, blocking collectives: 24 us -> none  [on_device(): tables = lax.all_gather(tables, 'dp', axis=0, tiled=True)]
    ppermute x0 -> x3, waiting for transfers between devices: none -> 19.3 us  [grow_blocks(): lax.ppermute(blocks, axis, [(i, i ^ bit) for i in range(size)])]
    ppermute x0 -> x3, starting transfers between devices: none -> 3.64 us  [grow_blocks(): lax.ppermute(blocks, axis, [(i, i ^ bit) for i in range(size)])]
  transfers between devices with their start and end apart: 5 -> 8, of which waited for: 4 -> 6; matrix products, arithmetic and copies ran while one was open for 4% -> 5% of each run, Pallas kernels for 0% -> 0%
where the time goes in v1:
time: 218 us; the launch traced here: 217 us
  waiting for transfers between devices  140 us (64%)
  matrix products  23.2 us (11%)
  between operations  14 us (6%)
  blocking collectives  13.5 us (6%)
  local copies, waits for them, and re-layouts  12.6 us (6%)
  starting transfers between devices  11 us (5%)
  other arithmetic  2.6 us (1%)
    reduce_scatter x1, waiting for transfers between devices, on_device(): lax.psum_scatter(partial, 'dp', scatter_dimension=0, tiled=True)  58.2 us
    all_gather x1, waiting for transfers between devices, on_device(): wide = lax.all_gather(normed, 'mp', axis=1, tiled=True)  34.2 us
    ppermute x3, waiting for transfers between devices, grow_blocks(): lax.ppermute(blocks, axis, [(i, i ^ bit) for i in range(size)])  19.3 us
    reduce_scatter x1, waiting for transfers between devices, on_device(): lax.psum_scatter(partial_value.astype(jnp.bfloat16), 'mp', scatter_dimens...  16 us
    psum x1, blocking collectives, on_device(): sums = lax.psum(sums, 'mp') / (feat_local * mp_count)  13.5 us
    all_to_all x1, waiting for transfers between devices, on_device(): lax.all_to_all(outgoing.reshape(pack_count, capacity, feat_local), 'dp',...  12.4 us
    dot_general x1, matrix products, on_device(): jnp.dot(ordered, qkv_weight.reshape(qkv_weight.shape[0], local_cols), pre...  12.2 us
    unnamed x18, local copies, waits for them, and re-layouts  10.7 us
  transfers between devices with their start and end apart: 8, of which 6 were waited for; matrix products, arithmetic and copies ran while one was open for 5% of the time, Pallas kernels for 0%

profile of v1, /device:TPU:0, one launch (start us, length us, event | category | flops | bytes accessed | tf_op | source)
XLA Modules:
  0.0 217.0 jit_solution(14200700429404013596)
XLA Ops:
  7.2 1.2 copy.33
  8.7 13.5 %psum.7 = f32[2,128]{1,0:T(2,128)S(1)} all-reduce(f32[2,128]{1,0:T(2,128)S(1)} %pad_maximum_fusion), channel_id=1, replica_groups=mesh['dp'=8,'mp'=4] {'mp'}, use_global_device_ids=true, to_apply=%region_3.4 | all-reduce | flops 256 | bytes 2048 | tf_op jit(solution)/shard_map/psum | solution.py:55
  22.2 0.8 dynamic_slice.3
  23.0 1.0 fusion.8
  24.1 1.1 collective-permute-done
  25.3 34.2 %all-gather.2.cloned.1.call-done = bf16[128,6144]{0,1:T(8,128)(2,1)} async-done(((bf16[128,1536]{0,1:T(8,128)(2,1)}), bf16[128,6144]{0,1:T(8,128)(2,1)}) %all-gather.2.cloned.1.call-update) | async-done | bytes 1572880 | tf_op jit(solution)/shard_map/all_gather | solution.py:60
  59.5 3.7 %all-to-all-start.1 = ((bf16[128,8,768]{0,2,1:T(8,128)(2,1)}), bf16[128,8,768]{0,2,1:T(8,128)(2,1)S(1)}, u32[]{:S(2)}, u32[]{:S(2)}) async-start(bf16[128,8,768]{0,2,1:T(8,128)(2,1)} %bitcast.83), calls=%async_computation.1 | async-start | bytes 3145728 | tf_op jit(solution)/shard_map/all_to_all | solution.py:61
  63.2 2.0 collective-permute-start.1
  65.2 18.1 %collective-permute-done.1 = s32[2,1,3,8]{3,2,1,0:T(4,128)S(1)} collective-permute-done((s32[2,1,3,8]{3,2,1,0:T(4,128)S(1)}, s32[2,1,3,8]{3,2,1,0:T(4,128)S(1)}, u32[]{:S(2)}, u32[]{:S(2)}) %collective-permute-start.1) | collective-permute-done | bytes 224 | tf_op jit(solution)/shard_map/ppermute | solution.py:19
  83.4 1.5 collective-permute-start.2
  84.9 6.7 %copy.35 = bf16[768,3,1024]{0,2,1:T(8,128)(2,1)} copy(bf16[768,3,1024]{2,0,1:T(8,128)(2,1)} %param.16) | data formatting | bytes 9437184 | tf_op args[6]
  91.9 0.7 copy.34
  92.6 12.2 %convolution_convert_fusion.1 = bf16[1024,3072]{1,0:T(8,128)(2,1)} fusion(bf16[768,3072]{0,1:T(8,128)(2,1)} %bitcast.79, bf16[1024,768]{1,0:T(8,128)(2,1)S(1)} %bitcast.84, s32[1024]{0:T(1024)S(1)} %bitcast.93), kind=kOutput, calls=%fused_computation.1 | convolution fusion | flops 6447431680 | bytes 12587008 | tf_op jit(solution)/shard_map/dot_general | solution.py:70
  104.9 0.6 copy-done.3
  105.6 58.2 %reduce-scatter.3.cloned.1.call-done = bf16[128,3072]{1,0:T(8,128)(2,1)} async-done(((bf16[1024,3072]{1,0:T(8,128)(2,1)}), bf16[128,3072]{1,0:T(8,128)(2,1)}) %reduce-scatter.3.cloned.1.call-update) | async-done | bytes 786448 | tf_op jit(solution)/shard_map/reduce_scatter | solution.py:75
  163.9 1.3 copy.41
  166.4 0.7 fusion.4
  167.4 7.6 %convolution_convert_fusion = bf16[128,6144]{1,0:T(8,128)(2,1)} fusion(bf16[128,1024]{0,1:T(8,128)(2,1)S(1)} %bitcast.86, bf16[1024,6144]{1,0:T(8,128)(2,1)} %param.19), kind=kOutput, calls=%fused_computation | convolution fusion | flops 1611399168 | bytes 14417920 | tf_op jit(solution)/shard_map/dot_general | solution.py:112
  175.3 0.7 copy-done
  176.0 1.3 convolution_convert_fusion.2
  177.3 3.5 %all-to-all-start = ((bf16[8,32,1536]{2,1,0:T(8,128)(2,1)}), bf16[8,32,1536]{2,1,0:T(8,128)(2,1)S(1)}, u32[]{:S(2)}, u32[]{:S(2)}) async-start(bf16[8,32,1536]{2,1,0:T(8,128)(2,1)} %bitcast.3), calls=%async_computation | async-start | bytes 1572864 | tf_op jit(solution)/shard_map/all_to_all | solution.py:82
  181.0 12.4 %all-to-all-done = bf16[8,32,1536]{2,1,0:T(8,128)(2,1)S(1)} async-done(((bf16[8,32,1536]{2,1,0:T(8,128)(2,1)}), bf16[8,32,1536]{2,1,0:T(8,128)(2,1)S(1)}, u32[]{:S(2)}, u32[]{:S(2)}) %all-to-all-start) | async-done | bytes 786464 | tf_op jit(solution)/shard_map/all_to_all | solution.py:82
  193.4 1.0 convolution_convert_fusion.3
  194.4 16.0 %reduce-scatter.5.cloned.1.call-done = bf16[128,1536]{1,0:T(8,128)(2,1)} async-done(((bf16[128,6144]{1,0:T(8,128)(2,1)}), bf16[128,1536]{1,0:T(8,128)(2,1)}) %reduce-scatter.5.cloned.1.call-update) | async-done | bytes 393232 | tf_op jit(solution)/shard_map/reduce_scatter | solution.py:113
  (53 shorter events, 2.8 us)
Async XLA Ops:
  7.2 16.8 %copy-start.1 = (s32[1,8]{1,0:T(1,128)S(1)}, s32[1,8]{1,0:T(1,128)}, u32[]{:S(2)}) copy-start(s32[1,8]{1,0:T(1,128)} %param.11) | copy-start | bytes 100
  7.2 16.8 %copy-start.4 = (s32[1,8]{1,0:T(1,128)S(1)}, s32[1,8]{1,0:T(1,128)}, u32[]{:S(2)}) copy-start(s32[1,8]{1,0:T(1,128)} %param.12) | copy-start | bytes 100
  7.2 16.8 %copy-start.2 = (s32[1,8]{1,0:T(1,128)S(1)}, s32[1,8]{1,0:T(1,128)}, u32[]{:S(2)}) copy-start(s32[1,8]{1,0:T(1,128)} %param.13) | copy-start | bytes 100
  7.2 52.3 %all-gather.2.cloned.1.call-start = ((), (), s32[]{:S(2)}) async-start(), calls=%async_computation.4 | async-start | bytes 1966080 | tf_op jit(solution)/shard_map/all_gather | solution.py:60
  24.1 1.2 collective-permute-start
  59.5 32.4 %all-to-all-start.1 = ((bf16[128,8,768]{0,2,1:T(8,128)(2,1)}), bf16[128,8,768]{0,2,1:T(8,128)(2,1)S(1)}, u32[]{:S(2)}, u32[]{:S(2)}) async-start(bf16[128,8,768]{0,2,1:T(8,128)(2,1)} %bitcast.83), calls=%async_computation.1 | async-start | bytes 3145728 | tf_op jit(solution)/shard_map/all_to_all | solution.py:61
  63.1 100.7 %reduce-scatter.3.cloned.1.call-start = ((), (), s32[]{:S(2)}) async-start(), calls=%async_computation.5 | async-start | bytes 7077888 | tf_op jit(solution)/shard_map/reduce_scatter | solution.py:75
  63.2 20.2 %collective-permute-start.1 = (s32[2,1,3,8]{3,2,1,0:T(4,128)S(1)}, s32[2,1,3,8]{3,2,1,0:T(4,128)S(1)}, u32[]{:S(2)}, u32[]{:S(2)}) collective-permute-start(s32[2,1,3,8]{3,2,1,0:T(4,128)S(1)} %pad_add_fusion.1), channel_id=1, source_target_pairs={{0,8},{4,12},{8,0},{12,4},{16,24},{20,28},{24,16},{28,20},{1,9},{5... | collective-permute-start | bytes 584 | tf_op jit(solution)/shard_map/ppermute | solution.py:19
  83.4 8.3 %collective-permute-start.2 = (s32[4,1,3,8]{3,2,1,0:T(4,128)S(1)}, s32[4,1,3,8]{3,2,1,0:T(4,128)S(1)}, u32[]{:S(2)}, u32[]{:S(2)}) collective-permute-start(s32[4,1,3,8]{3,2,1,0:T(4,128)S(1)} %pad_add_fusion), channel_id=1, source_target_pairs={{0,16},{4,20},{8,24},{12,28},{16,0},{20,4},{24,8},{28,12},{1,17},{... | collective-permute-start | bytes 1160 | tf_op jit(solution)/shard_map/ppermute | solution.py:19
  104.9 0.7 copy-start.3
  104.9 105.5 %reduce-scatter.5.cloned.1.call-start = ((), (), s32[]{:S(2)}) async-start(), calls=%async_computation.6 | async-start | bytes 1966080 | tf_op jit(solution)/shard_map/reduce_scatter | solution.py:113
  165.3 1.0 copy-start.5
  165.3 1.0 copy-start.6
  175.0 1.0 copy-start
  177.3 16.1 %all-to-all-start = ((bf16[8,32,1536]{2,1,0:T(8,128)(2,1)}), bf16[8,32,1536]{2,1,0:T(8,128)(2,1)S(1)}, u32[]{:S(2)}, u32[]{:S(2)}) async-start(bf16[8,32,1536]{2,1,0:T(8,128)(2,1)} %bitcast.3), calls=%async_computation | async-start | bytes 1572864 | tf_op jit(solution)/shard_map/all_to_all | solution.py:82
Sparse Core Ops, SparseCore 0:
  24.1 35.2 all-gather.1
  105.0 58.7 reduce-scatter.2
  175.1 35.2 reduce-scatter.4
